TPU v7x, 32 devices: a whole 2x2x4 slice. The times are simulated.
32 devices in a mesh: depth: 4 (over y, x), surf: 8 (over z, core).
Axes of the slice: x: 2, y: 2, z: 4, core: 2. Of those that a mesh axis runs over, the one named last changes fastest.
Arguments:
- initial_warmth: float32 [256, 32, 2048], P('depth', 'surf'), may hold values from -6 to 6
- substance_label: int32 [256], replicated, may hold values from 0 to 3, never falling along the last dimension, each value on 1 to 128 neighbouring positions
- neighbour_kernel: float32 [4, 24], replicated, may hold values from 0.004 to 0.04
- arriving_heat_rate: float32 [32, 2048], P('surf'), may hold values from -3 to 3
- implicit_inverse_operator: float32 [256, 256], replicated, may hold values from 0 to 0.61, as said below
Outputs:
- final_temperature: float32 [256, 32, 2048], P('depth', 'surf')
Inputs may be any that keep to these rules, and one draw needn't show every extreme that they name: `substance_label`: material numbers never fall from layer 0 (the heated side) to the last layer; every material holds at least one layer. `implicit_inverse_operator`: all entries are positive.
All inputs are finite; a program needn't handle non-finite values.
Results may differ from a plain program's by a relative error of at most 0.0001.
Values sent between devices are 32-bit elements; how exact they have to be, the bound alone decides.
A program may use at most 64 MiB of HBM per device.

v0:
```python
import jax
import jax.numpy as jnp
from jax import lax
from jax.sharding import PartitionSpec as P

STEPS = 3


neighbours = [
    (row_step, column_stride)
    for row_step in range(-2, 3)
    for column_stride in range(-2, 3)
    if row_step != 0 or column_stride != 0
]


def with_halo(cells, sides, width):
    for axis, dim in sides:
        count = lax.axis_size(axis)
        ends = count - 1
        head = lax.slice_in_dim(cells, 0, width, axis=dim)
        tail = lax.slice_in_dim(cells, cells.shape[dim] - width, cells.shape[dim], axis=dim)
        cells = jnp.concatenate(
            [
                lax.ppermute(tail, axis, [(i, (i + 1) % count) for i in range(ends)]),
                cells,
                lax.ppermute(head, axis, [((i + 1) % count, i) for i in range(ends)]),
            ],
            axis=dim,
        )
    return cells


def coefficients(substance_label, neighbour_kernel):
    chosen = (substance_label[:, None] == jnp.arange(4, dtype=jnp.int32)[None, :]).astype(
        neighbour_kernel.dtype
    )
    return jnp.sum(chosen[:, :, None] * neighbour_kernel[None, :, :], axis=1)


def lateral_diffusion(bordered_field, current_thermal_state, kernel_factors):
    tally_lines = current_thermal_state.shape[1]
    grid_breadth = current_thermal_state.shape[2]
    accumulated = jnp.zeros_like(current_thermal_state)
    for place_index, offset in enumerate(neighbours):
        displaced_field = bordered_field[
            :,
            2 + offset[0] : 2 + offset[0] + tally_lines,
            2 + offset[1] : 2 + offset[1] + grid_breadth,
        ]
        accumulated = accumulated + kernel_factors[:, place_index][:, None, None] * (
            displaced_field - current_thermal_state
        )
    return current_thermal_state + accumulated


def combine_plies(implicit_inverse_operator, advance_explicit_step):
    return jnp.einsum(
        "mq,qhl->mhl",
        implicit_inverse_operator,
        advance_explicit_step,
        precision=lax.Precision.HIGHEST,
        preferred_element_type=jnp.float32,
    )


def shards(
    initial_warmth, substance_label, neighbour_kernel, arriving_heat_rate, implicit_inverse_operator
):
    depth_count = lax.axis_size("depth")
    tile_span_across = initial_warmth.shape[2] // depth_count
    depth_rank = lax.axis_index("depth")
    sheet_factors = coefficients(substance_label, neighbour_kernel)
    current_thermal_state = lax.all_to_all(
        initial_warmth, "depth", split_axis=2, concat_axis=0, tiled=True
    )
    block_flux = lax.dynamic_slice_in_dim(
        arriving_heat_rate, depth_rank * tile_span_across, tile_span_across, 1
    )
    for step_index in range(STEPS):
        bordered_field = with_halo(current_thermal_state, (("depth", 2), ("surf", 1)), 2)
        advance_explicit_step = lateral_diffusion(
            bordered_field, current_thermal_state, sheet_factors
        )
        advance_explicit_step = advance_explicit_step.at[0].add(block_flux)
        current_thermal_state = combine_plies(implicit_inverse_operator, advance_explicit_step)
    return lax.all_to_all(current_thermal_state, "depth", split_axis=0, concat_axis=2, tiled=True)


def solution(mesh):
    return jax.shard_map(
        shards,
        mesh=mesh,
        in_specs=(P("depth", "surf", None), P(), P(), P("surf", None), P()),
        out_specs=P("depth", "surf", None),
        check_vma=False,
    )
```

profile of v0, /device:TPU:16, one launch (start us, length us, event | category | flops | bytes accessed | tf_op | source)
XLA Modules:
  0.0 233.7 jit_solution(5113391773547259741)
XLA Ops:
  0.0 4.8 %copy.184 = f32[64,4,2048]{0,1,2:T(4,128)} copy(f32[64,4,2048]{2,1,0:T(4,128)} %param.11) | data formatting | bytes 4194304 | tf_op args[0]
  4.8 5.5 %reshape.131 = f32[4,1,131072]{2,1,0:T(1,128)S(1)} reshape(f32[2048,4,64]{2,1,0:T(4,128)} %bitcast.53) | data formatting | bytes 4194304
  10.3 29.0 %all_to_all.36 = f32[4,1,131072]{2,1,0:T(1,128)} all-to-all(f32[4,1,131072]{2,1,0:T(1,128)S(1)} %reshape.131), channel_id=1, replica_groups=mesh['depth'=4,'surf'=8] {'depth'}, dimensions={0} | all-to-all | bytes 4194304 | tf_op jit(solution)/shard_map/all_to_all | solution.py:74
  39.3 0.5 broadcast.62
  39.8 7.7 %reduce.6 = f32[4,131072]{1,0:T(4,128)S(1)} reduce(f32[4,1,131072]{2,1,0:T(1,128)} %all_to_all.36, f32[]{:T(128)} %broadcast.62), dimensions={1}, to_apply=%all_to_all.26.reduce_sub_computation | reduce | bytes 4194308 | tf_op jit(solution)/shard_map/all_to_all | solution.py:74
  47.5 4.8 %reshape.132 = f32[2048,4,64]{2,1,0:T(4,128)} reshape(f32[4,131072]{1,0:T(4,128)S(1)} %reduce.6) | data formatting | bytes 4194304
  52.4 4.7 %copy.186 = f32[4,64,4,512]{3,1,0,2:T(8,128)} copy(f32[4,64,4,512]{1,2,3,0:T(4,128)} %bitcast.52) | data formatting | bytes 4194304 | tf_op jit(solution)/shard_map/all_to_all | solution.py:74
  57.1 1.9 copy.220
  59.0 2.8 %collective-permute-start = (f32[256,4,2]{0,2,1:T(2,128)S(1)}, f32[256,4,2]{0,2,1:T(2,128)S(1)}, u32[]{:S(2)}, u32[]{:S(2)}) collective-permute-start(f32[256,4,2]{0,2,1:T(2,128)S(1)} %get-tuple-element.57), channel_id=1, source_target_pairs={{0,8},{8,16},{16,24},{1,9},{9,17},{17,25},{2,10},{10,18},{18,26},{... | collective-permute-start | bytes 24584 | tf_op jit(solution)/shard_map/ppermute | solution.py:25
  61.9 1.5 collective-permute-start.1
  63.4 4.1 %collective-permute-done.1 = f32[256,4,2]{0,2,1:T(2,128)S(1)} collective-permute-done((f32[256,4,2]{0,2,1:T(2,128)S(1)}, f32[256,4,2]{0,2,1:T(2,128)S(1)}, u32[]{:S(2)}, u32[]{:S(2)}) %collective-permute-start.1) | collective-permute-done | bytes 8224 | tf_op jit(solution)/shard_map/ppermute | solution.py:27
  67.4 0.2 pad_maximum_fusion.3
  67.6 0.2 fusion.168
  67.8 1.5 copy.208
  69.3 2.0 collective-permute-start.3
  71.3 1.5 copy.190
  72.9 2.4 %collective-permute-start.2 = (f32[256,2,516]{0,1,2:T(2,128)}, f32[256,2,516]{0,1,2:T(2,128)}, u32[]{:S(2)}, u32[]{:S(2)}) collective-permute-start(f32[256,2,516]{0,1,2:T(2,128)} %copy.190), channel_id=1, source_target_pairs={{0,1},{1,2},{2,3},{3,4},{4,5},{5,6},{6,7},{8,9},{9,10},{10,11},{11... | collective-permute-start | bytes 3170312 | tf_op jit(solution)/shard_map/ppermute | solution.py:25
  75.3 0.7 dynamic-slice_bitcast_fusion
  76.0 0.4 copy.221
  76.5 7.5 %collective-permute-done.3 = f32[256,2,516]{0,1,2:T(2,128)} collective-permute-done((f32[256,2,516]{0,1,2:T(2,128)}, f32[256,2,516]{0,1,2:T(2,128)}, u32[]{:S(2)}, u32[]{:S(2)}) %collective-permute-start.3) | collective-permute-done | bytes 1056800 | tf_op jit(solution)/shard_map/ppermute | solution.py:27
  84.0 1.3 copy.209
  85.4 4.0 %collective-permute-done.2 = f32[256,2,516]{0,1,2:T(2,128)} collective-permute-done((f32[256,2,516]{0,1,2:T(2,128)}, f32[256,2,516]{0,1,2:T(2,128)}, u32[]{:S(2)}, u32[]{:S(2)}) %collective-permute-start.2) | collective-permute-done | bytes 1056800 | tf_op jit(solution)/shard_map/ppermute | solution.py:25
  89.4 1.3 copy.191
  90.7 0.7 maximum_maximum_fusion
  91.4 8.0 %fusion.57 = f32[256,4,512]{0,2,1:T(8,128)S(1)} fusion(f32[256,4,512]{0,2,1:T(8,128)S(1)} %copy.220, f32[256,4,2]{0,2,1:T(2,128)S(1)} %collective-permute-done.1, f32[256,4,2]{0,2,1:T(2,128)S(1)} %collective-permute-done, f32[256,6,516]{0,2,1:T(8,128)S(1)} %get-tuple-element.52, f32[256,6,516]{0,2,1:T(8,128)S(1)} %get-tuple-element.51, f32[256]{0:T(256)S(1)} %bitcast.74, ...), kind=kLoop, calls=%fused_computation.78 | loop fusion | flops 39845888 | bytes 46178304 | tf_op jit(solution)/shard_map/add | solution.py:54
  99.4 1.3 copy-done.1
  100.9 3.4 %scatter-add.10 = f32[256,4,512]{0,2,1:T(8,128)} dynamic-update-slice(f32[256,4,512]{0,2,1:T(8,128)} %copy-done.1, f32[1,4,512]{0,2,1:T(8,128)S(1)} %slice_add_fusion.2, s32[]{:T(128)} %constant.75.clone.1, s32[]{:T(128)} %constant.75.clone.1, s32[]{:T(128)} %constant.75.clone.1) | dynamic-update-slice | bytes 16388 | tf_op jit(solution)/shard_map/scatter-add | solution.py:85
  104.3 3.5 %convolution_bitcast_fusion.2 = f32[256,4,512]{0,2,1:T(8,128)S(1)} fusion(f32[256,4,512]{0,2,1:T(8,128)} %scatter-add.10, f32[256,256]{1,0:T(8,128)S(1)} %copy-done), kind=kOutput, calls=%fused_computation.251 | convolution fusion | flops 1610612736 | bytes 4456448 | tf_op jit(solution)/shard_map/mq,qhl->mhl/dot_general | solution.py:58
  107.8 4.3 %collective-permute-start.4 = (f32[256,4,2]{0,2,1:T(2,128)S(1)}, f32[256,4,2]{0,2,1:T(2,128)S(1)}, u32[]{:S(2)}, u32[]{:S(2)}) collective-permute-start(f32[256,4,2]{0,2,1:T(2,128)S(1)} %get-tuple-element.55), channel_id=1, source_target_pairs={{0,8},{8,16},{16,24},{1,9},{9,17},{17,25},{2,10},{10,18},{18,26},{... | collective-permute-start | bytes 24584 | tf_op jit(solution)/shard_map/ppermute | solution.py:25
  112.1 1.3 collective-permute-start.5
  113.4 4.2 %collective-permute-done.5 = f32[256,4,2]{0,2,1:T(2,128)S(1)} collective-permute-done((f32[256,4,2]{0,2,1:T(2,128)S(1)}, f32[256,4,2]{0,2,1:T(2,128)S(1)}, u32[]{:S(2)}, u32[]{:S(2)}) %collective-permute-start.5) | collective-permute-done | bytes 8224 | tf_op jit(solution)/shard_map/ppermute | solution.py:27
  117.6 0.2 pad_maximum_fusion.4
  117.8 0.2 fusion.167
  118.0 0.5 copy.224
  118.6 1.9 collective-permute-start.7
  120.5 0.5 copy.222
  121.0 2.4 %collective-permute-start.6 = (f32[256,2,516]{0,1,2:T(2,128)S(1)}, f32[256,2,516]{0,1,2:T(2,128)S(1)}, u32[]{:S(2)}, u32[]{:S(2)}) collective-permute-start(f32[256,2,516]{0,1,2:T(2,128)S(1)} %copy.222), channel_id=1, source_target_pairs={{0,1},{1,2},{2,3},{3,4},{4,5},{5,6},{6,7},{8,9},{9,10},{10,11},{11... | collective-permute-start | bytes 3170312 | tf_op jit(solution)/shard_map/ppermute | solution.py:25
  123.5 9.4 %collective-permute-done.7 = f32[256,2,516]{0,1,2:T(2,128)S(1)} collective-permute-done((f32[256,2,516]{0,1,2:T(2,128)S(1)}, f32[256,2,516]{0,1,2:T(2,128)S(1)}, u32[]{:S(2)}, u32[]{:S(2)}) %collective-permute-start.7) | collective-permute-done | bytes 1056800 | tf_op jit(solution)/shard_map/ppermute | solution.py:27
  133.0 4.3 %collective-permute-done.6 = f32[256,2,516]{0,1,2:T(2,128)S(1)} collective-permute-done((f32[256,2,516]{0,1,2:T(2,128)S(1)}, f32[256,2,516]{0,1,2:T(2,128)S(1)}, u32[]{:S(2)}, u32[]{:S(2)}) %collective-permute-start.6) | collective-permute-done | bytes 1056800 | tf_op jit(solution)/shard_map/ppermute | solution.py:25
  137.3 0.6 maximum_maximum_fusion.1
  138.0 8.0 %fusion.36 = f32[256,4,512]{0,2,1:T(8,128)S(1)} fusion(f32[256,4,512]{0,2,1:T(8,128)S(1)} %convolution_bitcast_fusion.2, f32[256,4,2]{0,2,1:T(2,128)S(1)} %collective-permute-done.5, f32[256,4,2]{0,2,1:T(2,128)S(1)} %collective-permute-done.4, f32[256,6,516]{0,2,1:T(8,128)S(1)} %get-tuple-element.50, f32[256,6,516]{0,2,1:T(8,128)S(1)} %get-tuple-element.49, ...), kind=kLoop, calls=%fused_computation.57 | loop fusion | flops 39845888 | bytes 46178304 | tf_op jit(solution)/shard_map/add | solution.py:54
  146.0 1.1 slice_add_fusion.1
  147.1 4.6 %scatter-add.11 = f32[256,4,512]{0,2,1:T(8,128)S(1)} dynamic-update-slice(f32[256,4,512]{0,2,1:T(8,128)S(1)} %fusion.36, f32[1,4,512]{0,2,1:T(8,128)} %slice_add_fusion.1, s32[]{:T(128)} %constant.75.clone.1, s32[]{:T(128)} %constant.75.clone.1, s32[]{:T(128)} %constant.75.clone.1) | dynamic-update-slice | bytes 16388 | tf_op jit(solution)/shard_map/scatter-add | solution.py:85
  151.7 1.9 convolution_bitcast_fusion.1
  153.6 2.8 %collective-permute-start.8 = (f32[256,4,2]{0,2,1:T(2,128)S(1)}, f32[256,4,2]{0,2,1:T(2,128)S(1)}, u32[]{:S(2)}, u32[]{:S(2)}) collective-permute-start(f32[256,4,2]{0,2,1:T(2,128)S(1)} %get-tuple-element.53), channel_id=1, source_target_pairs={{0,8},{8,16},{16,24},{1,9},{9,17},{17,25},{2,10},{10,18},{18,26},{... | collective-permute-start | bytes 24584 | tf_op jit(solution)/shard_map/ppermute | solution.py:25
  156.4 1.5 collective-permute-start.9
  158.0 4.0 %collective-permute-done.9 = f32[256,4,2]{0,2,1:T(2,128)S(1)} collective-permute-done((f32[256,4,2]{0,2,1:T(2,128)S(1)}, f32[256,4,2]{0,2,1:T(2,128)S(1)}, u32[]{:S(2)}, u32[]{:S(2)}) %collective-permute-start.9) | collective-permute-done | bytes 8224 | tf_op jit(solution)/shard_map/ppermute | solution.py:27
  162.0 0.2 pad_maximum_fusion.5
  162.4 0.5 copy.229
  162.9 1.9 collective-permute-start.11
  164.8 0.5 copy.227
  165.4 2.4 %collective-permute-start.10 = (f32[256,2,516]{0,1,2:T(2,128)S(1)}, f32[256,2,516]{0,1,2:T(2,128)S(1)}, u32[]{:S(2)}, u32[]{:S(2)}) collective-permute-start(f32[256,2,516]{0,1,2:T(2,128)S(1)} %copy.227), channel_id=1, source_target_pairs={{0,1},{1,2},{2,3},{3,4},{4,5},{5,6},{6,7},{8,9},{9,10},{10,11},{11... | collective-permute-start | bytes 3170312 | tf_op jit(solution)/shard_map/ppermute | solution.py:25
  167.8 9.4 %collective-permute-done.11 = f32[256,2,516]{0,1,2:T(2,128)S(1)} collective-permute-done((f32[256,2,516]{0,1,2:T(2,128)S(1)}, f32[256,2,516]{0,1,2:T(2,128)S(1)}, u32[]{:S(2)}, u32[]{:S(2)}) %collective-permute-start.11) | collective-permute-done | bytes 1056800 | tf_op jit(solution)/shard_map/ppermute | solution.py:27
  177.3 4.3 %collective-permute-done.10 = f32[256,2,516]{0,1,2:T(2,128)S(1)} collective-permute-done((f32[256,2,516]{0,1,2:T(2,128)S(1)}, f32[256,2,516]{0,1,2:T(2,128)S(1)}, u32[]{:S(2)}, u32[]{:S(2)}) %collective-permute-start.10) | collective-permute-done | bytes 1056800 | tf_op jit(solution)/shard_map/ppermute | solution.py:25
  181.7 0.6 maximum_maximum_fusion.2
  182.3 8.0 %fusion.15 = f32[256,4,512]{0,2,1:T(8,128)S(1)} fusion(f32[256,4,512]{0,2,1:T(8,128)S(1)} %convolution_bitcast_fusion.1, f32[256,4,2]{0,2,1:T(2,128)S(1)} %collective-permute-done.9, f32[256,4,2]{0,2,1:T(2,128)S(1)} %collective-permute-done.8, f32[256,6,516]{0,2,1:T(8,128)S(1)} %get-tuple-element.48, f32[256,6,516]{0,2,1:T(8,128)S(1)} %get-tuple-element.47, ...), kind=kLoop, calls=%fused_computation.36 | loop fusion | flops 39845888 | bytes 46178304 | tf_op jit(solution)/shard_map/add | solution.py:54
  190.4 1.1 slice_add_fusion
  191.4 4.6 %scatter-add.14 = f32[256,4,512]{0,2,1:T(8,128)S(1)} dynamic-update-slice(f32[256,4,512]{0,2,1:T(8,128)S(1)} %fusion.15, f32[1,4,512]{0,2,1:T(8,128)} %slice_add_fusion, s32[]{:T(128)} %constant.75.clone.1, s32[]{:T(128)} %constant.75.clone.1, s32[]{:T(128)} %constant.75.clone.1) | dynamic-update-slice | bytes 16388 | tf_op jit(solution)/shard_map/scatter-add | solution.py:85
  196.0 3.2 %convolution_bitcast_fusion = f32[256,4,512]{0,2,1:T(8,128)} fusion(f32[256,4,512]{0,2,1:T(8,128)S(1)} %scatter-add.14, f32[256,256]{1,0:T(8,128)S(1)} %copy-done), kind=kOutput, calls=%fused_computation.249 | convolution fusion | flops 1610612736 | bytes 4456448 | tf_op jit(solution)/shard_map/mq,qhl->mhl/dot_general | solution.py:58
  199.2 2.2 copy.232
  201.4 27.5 %all_to_all.37 = f32[256,4,512]{2,1,0:T(4,128)S(1)} all-to-all(f32[256,4,512]{2,1,0:T(4,128)S(1)} %copy.232), channel_id=1, replica_groups=mesh['depth'=4,'surf'=8] {'depth'}, dimensions={0} | all-to-all | bytes 4194304 | tf_op jit(solution)/shard_map/all_to_all | solution.py:87
  228.9 0.7 copy.233
  229.6 1.4 copy.238
  231.0 2.8 %reshape.130 = f32[64,4,2048]{2,1,0:T(4,128)} reshape(f32[64,4,4,512]{3,2,1,0:T(4,128)S(1)} %copy.238) | data formatting | bytes 4194304 | tf_op jit(solution)/shard_map/all_to_all | solution.py:87
  (23 shorter events, 0.8 us)
Async XLA Ops:
  0.0 104.3 %copy-start = (f32[256,256]{1,0:T(8,128)S(1)}, f32[256,256]{1,0:T(8,128)}, u32[]{:S(2)}) copy-start(f32[256,256]{1,0:T(8,128)} %param.15) | copy-start | bytes 786436
  59.0 4.3 %collective-permute-start = (f32[256,4,2]{0,2,1:T(2,128)S(1)}, f32[256,4,2]{0,2,1:T(2,128)S(1)}, u32[]{:S(2)}, u32[]{:S(2)}) collective-permute-start(f32[256,4,2]{0,2,1:T(2,128)S(1)} %get-tuple-element.57), channel_id=1, source_target_pairs={{0,8},{8,16},{16,24},{1,9},{9,17},{17,25},{2,10},{10,18},{18,26},{... | collective-permute-start | bytes 24584 | tf_op jit(solution)/shard_map/ppermute | solution.py:25
  61.9 5.5 %collective-permute-start.1 = (f32[256,4,2]{0,2,1:T(2,128)S(1)}, f32[256,4,2]{0,2,1:T(2,128)S(1)}, u32[]{:S(2)}, u32[]{:S(2)}) collective-permute-start(f32[256,4,2]{0,2,1:T(2,128)S(1)} %get-tuple-element.58), channel_id=1, source_target_pairs={{8,0},{16,8},{24,16},{9,1},{17,9},{25,17},{10,2},{18,10},{26,18},{... | collective-permute-start | bytes 24584 | tf_op jit(solution)/shard_map/ppermute | solution.py:27
  69.3 7.1 %copy-start.3 = (s32[256]{0:T(256)S(1)}, s32[256]{0:T(256)}, u32[]{:S(2)}) copy-start(s32[256]{0:T(256)} %param.12) | copy-start | bytes 3076
  69.3 7.1 %copy-start.2 = (f32[4,24]{1,0:T(4,128)S(1)}, f32[4,24]{1,0:T(4,128)}, u32[]{:S(2)}) copy-start(f32[4,24]{1,0:T(4,128)} %param.13) | copy-start | bytes 1156
  69.3 14.7 %collective-permute-start.3 = (f32[256,2,516]{0,1,2:T(2,128)}, f32[256,2,516]{0,1,2:T(2,128)}, u32[]{:S(2)}, u32[]{:S(2)}) collective-permute-start(f32[256,2,516]{0,1,2:T(2,128)} %copy.208), channel_id=1, source_target_pairs={{1,0},{2,1},{3,2},{4,3},{5,4},{6,5},{7,6},{9,8},{10,9},{11,10},{12... | collective-permute-start | bytes 3170312 | tf_op jit(solution)/shard_map/ppermute | solution.py:27
  72.9 16.5 %collective-permute-start.2 = (f32[256,2,516]{0,1,2:T(2,128)}, f32[256,2,516]{0,1,2:T(2,128)}, u32[]{:S(2)}, u32[]{:S(2)}) collective-permute-start(f32[256,2,516]{0,1,2:T(2,128)} %copy.190), channel_id=1, source_target_pairs={{0,1},{1,2},{2,3},{3,4},{4,5},{5,6},{6,7},{8,9},{9,10},{10,11},{11... | collective-permute-start | bytes 3170312 | tf_op jit(solution)/shard_map/ppermute | solution.py:25
  99.4 1.3 copy-start.1
  107.8 5.6 %collective-permute-start.4 = (f32[256,4,2]{0,2,1:T(2,128)S(1)}, f32[256,4,2]{0,2,1:T(2,128)S(1)}, u32[]{:S(2)}, u32[]{:S(2)}) collective-permute-start(f32[256,4,2]{0,2,1:T(2,128)S(1)} %get-tuple-element.55), channel_id=1, source_target_pairs={{0,8},{8,16},{16,24},{1,9},{9,17},{17,25},{2,10},{10,18},{18,26},{... | collective-permute-start | bytes 24584 | tf_op jit(solution)/shard_map/ppermute | solution.py:25
  112.1 5.5 %collective-permute-start.5 = (f32[256,4,2]{0,2,1:T(2,128)S(1)}, f32[256,4,2]{0,2,1:T(2,128)S(1)}, u32[]{:S(2)}, u32[]{:S(2)}) collective-permute-start(f32[256,4,2]{0,2,1:T(2,128)S(1)} %get-tuple-element.56), channel_id=1, source_target_pairs={{8,0},{16,8},{24,16},{9,1},{17,9},{25,17},{10,2},{18,10},{26,18},{... | collective-permute-start | bytes 24584 | tf_op jit(solution)/shard_map/ppermute | solution.py:27
  118.6 14.3 %collective-permute-start.7 = (f32[256,2,516]{0,1,2:T(2,128)S(1)}, f32[256,2,516]{0,1,2:T(2,128)S(1)}, u32[]{:S(2)}, u32[]{:S(2)}) collective-permute-start(f32[256,2,516]{0,1,2:T(2,128)S(1)} %copy.224), channel_id=1, source_target_pairs={{1,0},{2,1},{3,2},{4,3},{5,4},{6,5},{7,6},{9,8},{10,9},{11,10},{12... | collective-permute-start | bytes 3170312 | tf_op jit(solution)/shard_map/ppermute | solution.py:27
  121.0 16.2 %collective-permute-start.6 = (f32[256,2,516]{0,1,2:T(2,128)S(1)}, f32[256,2,516]{0,1,2:T(2,128)S(1)}, u32[]{:S(2)}, u32[]{:S(2)}) collective-permute-start(f32[256,2,516]{0,1,2:T(2,128)S(1)} %copy.222), channel_id=1, source_target_pairs={{0,1},{1,2},{2,3},{3,4},{4,5},{5,6},{6,7},{8,9},{9,10},{10,11},{11... | collective-permute-start | bytes 3170312 | tf_op jit(solution)/shard_map/ppermute | solution.py:25
  153.6 4.4 %collective-permute-start.8 = (f32[256,4,2]{0,2,1:T(2,128)S(1)}, f32[256,4,2]{0,2,1:T(2,128)S(1)}, u32[]{:S(2)}, u32[]{:S(2)}) collective-permute-start(f32[256,4,2]{0,2,1:T(2,128)S(1)} %get-tuple-element.53), channel_id=1, source_target_pairs={{0,8},{8,16},{16,24},{1,9},{9,17},{17,25},{2,10},{10,18},{18,26},{... | collective-permute-start | bytes 24584 | tf_op jit(solution)/shard_map/ppermute | solution.py:25
  156.4 5.5 %collective-permute-start.9 = (f32[256,4,2]{0,2,1:T(2,128)S(1)}, f32[256,4,2]{0,2,1:T(2,128)S(1)}, u32[]{:S(2)}, u32[]{:S(2)}) collective-permute-start(f32[256,4,2]{0,2,1:T(2,128)S(1)} %get-tuple-element.54), channel_id=1, source_target_pairs={{8,0},{16,8},{24,16},{9,1},{17,9},{25,17},{10,2},{18,10},{26,18},{... | collective-permute-start | bytes 24584 | tf_op jit(solution)/shard_map/ppermute | solution.py:27
  162.9 14.3 %collective-permute-start.11 = (f32[256,2,516]{0,1,2:T(2,128)S(1)}, f32[256,2,516]{0,1,2:T(2,128)S(1)}, u32[]{:S(2)}, u32[]{:S(2)}) collective-permute-start(f32[256,2,516]{0,1,2:T(2,128)S(1)} %copy.229), channel_id=1, source_target_pairs={{1,0},{2,1},{3,2},{4,3},{5,4},{6,5},{7,6},{9,8},{10,9},{11,10},{12... | collective-permute-start | bytes 3170312 | tf_op jit(solution)/shard_map/ppermute | solution.py:27
  165.4 16.2 %collective-permute-start.10 = (f32[256,2,516]{0,1,2:T(2,128)S(1)}, f32[256,2,516]{0,1,2:T(2,128)S(1)}, u32[]{:S(2)}, u32[]{:S(2)}) collective-permute-start(f32[256,2,516]{0,1,2:T(2,128)S(1)} %copy.227), channel_id=1, source_target_pairs={{0,1},{1,2},{2,3},{3,4},{4,5},{5,6},{6,7},{8,9},{9,10},{10,11},{11... | collective-permute-start | bytes 3170312 | tf_op jit(solution)/shard_map/ppermute | solution.py:25
where the time goes:
time: 235 us; the launch traced here: 234 us
  blocking collectives  56.5 us (24%)
  local copies, waits for them, and re-layouts  52.9 us (23%)
  waiting for transfers between devices  51.3 us (22%)
  other arithmetic  36.7 us (16%)
  starting transfers between devices  27.3 us (12%)
  matrix products  8.59 us (4%)
    ppermute x6, waiting for transfers between devices, with_halo(): lax.ppermute(head, axis, [((i + 1) % count, i) for i in range(ends)])  38.6 us
    all_to_all x1, blocking collectives, shards(): lax.all_to_all(initial_warmth, 'depth', split_axis=2, concat_axis=0, tile...  29 us
    all_to_all x1, blocking collectives, shards(): lax.all_to_all(current_thermal_state, 'depth', split_axis=0, concat_axis=...  27.5 us
    add x3, other arithmetic, lateral_diffusion(): return current_thermal_state + accumulated  24 us
    ppermute x6, starting transfers between devices, with_halo(): lax.ppermute(tail, axis, [(i, (i + 1) % count) for i in range(ends)])  17.1 us
    unnamed x11, local copies, waits for them, and re-layouts  16.4 us
    ppermute x6, waiting for transfers between devices, with_halo(): lax.ppermute(tail, axis, [(i, (i + 1) % count) for i in range(ends)])  12.7 us
    scatter-add x3, local copies, waits for them, and re-layouts, shards(): advance_explicit_step = advance_explicit_step.at[0].add(block_flux)  12.6 us
  transfers between devices with their start and end apart: 12, of which 9 were waited for; matrix products, arithmetic and copies ran while one was open for 2% of the time, Pallas kernels for 0%

commit v1 on v0

v1 whole, which is shorter than its diff:
```python
import functools

import jax
import jax.numpy as jnp
from jax import lax
from jax.experimental import pallas as pl
from jax.experimental.pallas import tpu as pltpu
from jax.sharding import PartitionSpec as P

LANES = 128
REACH = 6
MESH = pl.DeviceIdType.MESH


def flipped(rank, mask, count):
    out, bit = 0, 1
    while bit < count:
        mine = (rank // bit) % 2
        out = out + bit * ((1 - mine) if (mask // bit) % 2 else mine)
        bit *= 2
    return out


def kernel(
    nd, ns, tiles,
    x_ref, lab_ref, nk_ref, heat_ref, op_ref, out_ref,
    raw, eraw, eb, hb, s0, s1, s2, ex, ob, coef, op3,
    a_send, a_recv, a_loc, z_send, z_recv, ze_send, ze_recv,
    h_send, h_recv, x_send, x_recv, o_send, o_recv, o_loc,
):
    d = lax.axis_index("depth")
    s = lax.axis_index("surf")
    layers_here = x_ref.shape[0]
    layers = op_ref.shape[0]
    width = heat_ref.shape[1]
    cols = tiles * LANES
    ring = tiles + 1
    peers = [j for j in range(nd - 1, 0, -1)]
    has = (s > 0, s < ns - 1)
    near = (s - 1, s + 1)
    mine = pl.ds(pl.multiple_of(d * layers_here, 8), layers_here)

    barrier = pltpu.get_barrier_semaphore()
    for j in peers:
        pl.semaphore_signal(
            barrier, inc=1, device_id={"depth": flipped(d, j, nd)}, device_id_type=MESH
        )
    for side in range(2):
        @pl.when(has[side])
        def _():
            pl.semaphore_signal(
                barrier, inc=1, device_id={"surf": near[side]}, device_id_type=MESH
            )
    at_end = jnp.where(s > 0, 0, 1) + jnp.where(s < ns - 1, 0, 1)
    pl.semaphore_wait(barrier, nd + 1 - at_end)

    def block_cols(b, t):
        return pl.ds(pl.multiple_of(b * cols + t * LANES, LANES), LANES)

    def spread(j, t):
        p = flipped(d, j, nd)
        if t == tiles:
            src, dst = eb.at[p], eraw.at[1, mine]
        else:
            src, dst = x_ref.at[:, :, block_cols(p, t)], raw.at[1, t, mine]
        return pltpu.make_async_remote_copy(
            src, dst, a_send.at[j, t], a_recv.at[j, t],
            device_id={"depth": p}, device_id_type=MESH,
        )

    def keep(t):
        if t == tiles:
            return pltpu.make_async_copy(eb.at[d], eraw.at[1, mine], a_loc.at[t])
        return pltpu.make_async_copy(
            x_ref.at[:, :, block_cols(d, t)], raw.at[1, t, mine], a_loc.at[t]
        )

    def forward(side, t):
        if t == tiles:
            src, dst = eraw.at[1], eraw.at[2 - 2 * side]
            snd, rcv = ze_send.at[side], ze_recv.at[side]
        else:
            src, dst = raw.at[1, t], raw.at[2 - 2 * side, t]
            snd, rcv = z_send.at[side, t], z_recv.at[side, t]
        return pltpu.make_async_remote_copy(
            src, dst, snd, rcv, device_id={"surf": near[side]}, device_id_type=MESH
        )

    def heat_out(side):
        return pltpu.make_async_remote_copy(
            heat_ref, hb.at[1 - side], h_send.at[side], h_recv.at[side],
            device_id={"surf": near[side]}, device_id_type=MESH,
        )

    def trade(side, t):
        return pltpu.make_async_remote_copy(
            s2.at[t, pl.ds(2 + 2 * side, 2)], s2.at[t, pl.ds(6 - 6 * side, 2)],
            x_send.at[side, t], x_recv.at[side, t],
            device_id={"surf": near[side]}, device_id_type=MESH,
        )

    def give_back(j, t):
        p = flipped(d, j, nd)
        theirs = pl.ds(pl.multiple_of(p * layers_here, 8), layers_here)
        return pltpu.make_async_remote_copy(
            ob.at[t, theirs], out_ref.at[:, :, block_cols(d, t)],
            o_send.at[j, t], o_recv.at[j, t],
            device_id={"depth": p}, device_id_type=MESH,
        )

    def put_home(t):
        return pltpu.make_async_copy(
            ob.at[t, mine], out_ref.at[:, :, block_cols(d, t)], o_loc.at[t]
        )

    for j in peers:
        spread(j, 0).start()
    lane8 = lax.broadcasted_iota(jnp.int32, (8, LANES), 1)
    for b in range(nd):
        @pl.loop(0, layers_here // 8)
        def _(g):
            rows = pl.ds(pl.multiple_of(g * 8, 8), 8)
            packed = jnp.zeros((8, LANES), jnp.float32)
            for r in range(4):
                edge = jnp.zeros((8, LANES), jnp.float32)
                if b < nd - 1:
                    ahead = x_ref[rows, r, (b + 1) * cols:(b + 1) * cols + LANES]
                    edge = jnp.where(lane8 < REACH, ahead, edge)
                if b > 0:
                    behind = x_ref[rows, r, b * cols - LANES:b * cols]
                    edge = jnp.where(lane8 >= LANES - REACH, behind, edge)
                packed = packed + (pltpu.roll(edge, 16 * r, 1) if r else edge)
            eb[b, rows, :] = packed
    for t in [tiles] + list(range(1, tiles)):
        for j in peers:
            spread(j, t).start()
    for t in range(ring):
        keep(t).start()
    for side in range(2):
        @pl.when(has[side])
        def _():
            heat_out(side).start()

    @pl.loop(0, layers // 8)
    def _(g):
        rows = pl.ds(pl.multiple_of(g * 8, 8), 8)
        lab = lab_ref[rows, :]
        is0, is1, is2 = lab == 0, lab == 1, lab == 2
        total = jnp.zeros((8, LANES), jnp.float32)
        for k in range(24):
            c = jnp.where(
                is0, nk_ref[0, k],
                jnp.where(is1, nk_ref[1, k], jnp.where(is2, nk_ref[2, k], nk_ref[3, k])),
            )
            coef[k if k < 12 else k + 1, rows, :] = c
            total = total + c
        coef[12, rows, :] = 1.0 - total

    high = op_ref[...].astype(jnp.bfloat16)
    op3[:, 0:layers] = high
    op3[:, layers:2 * layers] = high
    op3[:, 2 * layers:] = (op_ref[...] - high.astype(jnp.float32)).astype(jnp.bfloat16)

    for side in range(2):
        @pl.when(jnp.logical_not(has[side]))
        def _():
            for t in range(ring):
                for r in range(2):
                    s2[t, 6 * side + r, :, :] = jnp.zeros((layers, LANES), jnp.float32)
                for r in range(4):
                    s0[t, 8 * side + r, :, :] = jnp.zeros((layers, LANES), jnp.float32)
            hb[side, :, :] = jnp.zeros((4, width), jnp.float32)

    for side in range(2):
        @pl.when(has[side])
        def _():
            heat_out(side).wait_send()
            heat_out(1 - side).wait_recv()

    row_keep = [jnp.where(h, 1.0, 0.0).astype(jnp.float32) for h in has]
    lane1 = lax.broadcasted_iota(jnp.int32, (1, LANES), 1)
    edge_keep = jnp.where(
        lane1 < REACH, jnp.where(d < nd - 1, 1.0, 0.0),
        jnp.where(lane1 >= LANES - REACH, jnp.where(d > 0, 1.0, 0.0), 0.0),
    ).astype(jnp.float32)

    def heat_row(row, t):
        if row < 0:
            src, r = hb.at[0], row + 4
        elif row > 3:
            src, r = hb.at[1], row - 4
        else:
            src, r = heat_ref, row
        if t < tiles:
            return src[r:r + 1, block_cols(d, t)]
        ahead = src[r:r + 1, block_cols(lax.rem(d + 1, nd), 0)]
        behind = src[r:r + 1, block_cols(lax.rem(d + nd - 1, nd), tiles - 1)]
        return jnp.where(lane1 < REACH, ahead, behind)

    def lateral(src, t, made, first):
        left, right = (t - 1) % ring, (t + 1) % ring

        @pl.loop(0, layers // 8)
        def _(g):
            rows = pl.ds(pl.multiple_of(g * 8, 8), 8)
            cs = [coef[k, rows, :] for k in range(25)]
            acc = [None] * made
            for i in range(made + 4):
                mid, lo, hi = src[t, i, rows, :], src[left, i, rows, :], src[right, i, rows, :]
                views = [
                    pltpu.roll(jnp.where(lane8 >= LANES - 2, lo, mid), 2, 1),
                    pltpu.roll(jnp.where(lane8 >= LANES - 1, lo, mid), 1, 1),
                    mid,
                    pltpu.roll(jnp.where(lane8 < 1, hi, mid), LANES - 1, 1),
                    pltpu.roll(jnp.where(lane8 < 2, hi, mid), LANES - 2, 1),
                ]
                for r in range(max(0, i - 4), min(made, i + 1)):
                    for q in range(5):
                        term = cs[(i - r) * 5 + q] * views[q]
                        acc[r] = term if acc[r] is None else acc[r] + term
            for r in range(made):
                ex[rows, r * LANES:(r + 1) * LANES] = acc[r]

        top = lax.broadcasted_iota(jnp.int32, (8, LANES), 0) == 0
        for r in range(made):
            lanes = slice(r * LANES, (r + 1) * LANES)
            heat = jnp.broadcast_to(heat_row(first + r, t), (8, LANES))
            ex[0:8, lanes] = ex[0:8, lanes] + jnp.where(top, heat, 0.0)

    def implicit(t, made, first, store):
        for pair in range(made // 2):
            e = ex[:, pair * 2 * LANES:(pair + 1) * 2 * LANES]
            if first < 0 and pair == 0:
                e = e * row_keep[0]
            if first < 0 and pair == made // 2 - 1:
                e = e * row_keep[1]
            if t == tiles:
                e = e * jnp.concatenate([edge_keep, edge_keep], axis=1)
            eh = e.astype(jnp.bfloat16)
            el = (e - eh.astype(jnp.float32)).astype(jnp.bfloat16)
            y = jnp.dot(
                op3[...], jnp.concatenate([eh, el, eh], axis=0),
                preferred_element_type=jnp.float32,
            )
            store(2 * pair, y[:, :LANES])
            store(2 * pair + 1, y[:, LANES:])

    done = set()
    arrival = [0, tiles] + list(range(1, tiles))

    def once(f):
        def g(t):
            if (f.__name__, t) not in done:
                done.add((f.__name__, t))
                f(t)
        return g

    @once
    def arrive(t):
        at = arrival.index(t)
        if at:
            arrive(arrival[at - 1])
        for j in peers:
            spread(j, t).wait_recv()
        keep(t).wait()
        for side in range(2):
            @pl.when(has[side])
            def _():
                forward(side, t).start()

    @once
    def unpack(t):
        at = arrival.index(t)
        arrive(arrival[min(at + 1, tiles)])

        def relayout(part):
            if t == tiles:
                @pl.loop(0, layers // 8)
                def _(g):
                    rows = pl.ds(pl.multiple_of(g * 8, 8), 8)
                    packed = eraw[part, rows, :]
                    wanted = jnp.logical_or(lane8 < REACH, lane8 >= LANES - REACH)
                    for r in range(4):
                        v = pltpu.roll(packed, LANES - 16 * r, 1) if r else packed
                        s0[t, 4 * part + r, rows, :] = jnp.where(wanted, v, 0.0)
            else:
                @pl.loop(0, layers // 8)
                def _(g):
                    rows = pl.ds(pl.multiple_of(g * 8, 8), 8)
                    for r in range(4):
                        s0[t, 4 * part + r, rows, :] = raw[part, t, rows, r, :]

        relayout(1)
        for side in range(2):
            @pl.when(has[side])
            def _():
                forward(1 - side, t).wait_recv()
                relayout(2 * side)

    @once
    def step1(t):
        for u in (t, (t - 1) % ring, (t + 1) % ring):
            unpack(u)
        lateral(s0, t, 8, -2)

        def store(r, y):
            s1[t, r, :, :] = y
        implicit(t, 8, -2, store)

    @once
    def step2(t):
        for u in ((t - 1) % ring, t, (t + 1) % ring):
            step1(u)
        lateral(s1, t, 4, 0)

        def store(r, y):
            s2[t, 2 + r, :, :] = y
        implicit(t, 4, 0, store)
        for side in range(2):
            @pl.when(has[side])
            def _():
                trade(side, t).start()

    @once
    def halo(t):
        for side in range(2):
            @pl.when(has[side])
            def _():
                trade(1 - side, t).wait_recv()

    @once
    def step3(t):
        around = (t, (t - 1) % ring, (t + 1) % ring)
        for u in around:
            step2(u)
        for u in around:
            halo(u)
        lateral(s2, t, 4, 0)

        def store(r, y):
            ob[t, :, r, :] = y
        implicit(t, 4, 0, store)
        for j in peers:
            give_back(j, t).start()
        put_home(t).start()

    order = list(range(1, tiles)) + [0]
    for t in order:
        step3(t)

    for t in order:
        for j in peers:
            give_back(j, t).wait()
        put_home(t).wait()
    for t in range(ring):
        for j in peers:
            spread(j, t).wait_send()
        for side in range(2):
            @pl.when(has[side])
            def _():
                forward(side, t).wait_send()
                trade(side, t).wait_send()


def shards(
    nd, ns,
    initial_warmth, substance_label, neighbour_kernel, arriving_heat_rate, implicit_inverse_operator,
):
    layers_here, rows, width = initial_warmth.shape
    layers = implicit_inverse_operator.shape[0]
    tiles = width // nd // LANES
    ring = tiles + 1
    labels = jnp.broadcast_to(substance_label[:, None], (layers, LANES))
    f32, dma = jnp.float32, pltpu.SemaphoreType.DMA
    vmem = pl.BlockSpec(memory_space=pltpu.VMEM)
    return pl.pallas_call(
        functools.partial(kernel, nd, ns, tiles),
        out_shape=jax.ShapeDtypeStruct(initial_warmth.shape, f32),
        in_specs=[vmem, vmem, pl.BlockSpec(memory_space=pltpu.SMEM), vmem, vmem],
        out_specs=pl.BlockSpec(memory_space=pl.ANY),
        scratch_shapes=[
            pltpu.VMEM((3, tiles, layers, rows, LANES), f32),
            pltpu.VMEM((3, layers, LANES), f32),
            pltpu.VMEM((nd, layers_here, LANES), f32),
            pltpu.VMEM((2, rows, width), f32),
            pltpu.VMEM((ring, 3 * rows, layers, LANES), f32),
            pltpu.VMEM((ring, 2 * rows, layers, LANES), f32),
            pltpu.VMEM((ring, 2 * rows, layers, LANES), f32),
            pltpu.VMEM((layers, 2 * rows * LANES), f32),
            pltpu.VMEM((tiles, layers, rows, LANES), f32),
            pltpu.VMEM((25, layers, LANES), f32),
            pltpu.VMEM((layers, 3 * layers), jnp.bfloat16),
            dma((nd, ring)), dma((nd, ring)), dma((ring,)),
            dma((2, tiles)), dma((2, tiles)), dma((2,)), dma((2,)),
            dma((2,)), dma((2,)), dma((2, ring)), dma((2, ring)),
            dma((nd, tiles)), dma((nd, tiles)), dma((tiles,)),
        ],
        compiler_params=pltpu.CompilerParams(
            collective_id=0, has_side_effects=True, vmem_limit_bytes=60 * 1024 * 1024
        ),
    )(initial_warmth, labels, neighbour_kernel, arriving_heat_rate, implicit_inverse_operator)


def solution(mesh):
    return jax.shard_map(
        functools.partial(shards, mesh.shape["depth"], mesh.shape["surf"]),
        mesh=mesh,
        in_specs=(P("depth", "surf", None), P(), P(), P("surf", None), P()),
        out_specs=P("depth", "surf", None),
        check_vma=False,
    )
```

time: 235 us -> 124 us (0.53)
  Pallas kernels: 0 us -> 119 us
  blocking collectives: 56.5 us -> 0 us
  waiting for transfers between devices: 51.3 us -> 0 us
  local copies, waits for them, and re-layouts: 52.9 us -> 4.59 us
  other arithmetic: 36.7 us -> 0 us
  starting transfers between devices: 27.3 us -> 0 us
  matrix products: 8.59 us -> 0 us
    pallas_call x0 -> x1, Pallas kernels: none -> 119 us  [shards(): pl.pallas_call(functools.partial(kernel, nd, ns, tiles), out_shape=jax.Sh...]
    all_to_all x2 -> x0, blocking collectives: 56.5 us -> none  [the longest x1 29 us: shards(): lax.all_to_all(initial_warmth, 'depth', split_axis=2, concat_axis=0, tile...]
    ppermute x12 -> x0, waiting for transfers between devices: 51.3 us -> none  [the longest x6 38.6 us: with_halo(): lax.ppermute(head, axis, [((i + 1) % count, i) for i in range(ends)])]
    ppermute x12 -> x0, starting transfers between devices: 27.3 us -> none  [the longest x6 17.1 us: with_halo(): lax.ppermute(tail, axis, [(i, (i + 1) % count) for i in range(ends)])]
    add x6 -> x0, other arithmetic: 26.3 us -> none  [the longest x3 24 us: lateral_diffusion(): return current_thermal_state + accumulated]
    unnamed x11 -> x1, local copies, waits for them, and re-layouts: 16.4 us -> 3.16 us
    scatter-add x3 -> x0, local copies, waits for them, and re-layouts: 12.6 us -> none  [shards(): advance_explicit_step = advance_explicit_step.at[0].add(block_flux)]
    all_to_all x6 -> x0, local copies, waits for them, and re-layouts: 12 us -> none  [the longest x3 7.18 us: shards(): lax.all_to_all(initial_warmth, 'depth', split_axis=2, concat_axis=0, tile...]
  transfers between devices with their start and end apart: 12 -> 0, of which waited for: 9 -> 0; matrix products, arithmetic and copies ran while one was open for 2% -> 0% of each run, Pallas kernels for 0% -> 0%
where the time goes in v1:
time: 124 us
  Pallas kernels  119 us (96%)
  local copies, waits for them, and re-layouts  4.59 us (4%)
    pallas_call x1, Pallas kernels, shards(): pl.pallas_call(functools.partial(kernel, nd, ns, tiles), out_shape=jax.Sh...  119 us
    unnamed x1, local copies, waits for them, and re-layouts  3.16 us

profile of v1, /device:TPU:16, one launch (start us, length us, event | category | flops | bytes accessed | tf_op | source)
XLA Modules:
  0.0 123.8 jit_solution(14201965440148013807)
XLA Ops:
  0.0 1.4 %broadcast_in_dim.2.lab_ref = s32[256,128]{1,0:T(8,128)} broadcast(s32[256]{0:T(256)} %param.6), dimensions={0} | broadcast | bytes 132096 | tf_op jit(solution)/shard_map/broadcast_in_dim | solution.py:373
  1.4 119.2 %shard_map.55 = f32[64,4,2048]{2,1,0:T(4,128)} custom-call(f32[64,4,2048]{2,1,0:T(4,128)} %x_ref.1, s32[256,128]{1,0:T(8,128)} %broadcast_in_dim.2.lab_ref, f32[4,24]{1,0:T(4,128)} %nk_ref.1, f32[4,2048]{1,0:T(4,128)} %heat_ref.1, f32[256,256]{1,0:T(8,128)} %op_ref.1), custom_call_target="tpu_custom_call" | custom-call | tf_op jit(solution)/shard_map/pallas_call | solution.py:376
  120.7 3.2 %copy.7 = f32[64,4,2048]{2,1,0:T(4,128)} copy(f32[64,4,2048]{2,1,0:T(4,128)} %shard_map.55) | data formatting | bytes 4194304

commit v2 on v1

--- a/solution.py
+++ b/solution.py
@@ -24,8 +24,8 @@
 def kernel(
     nd, ns, tiles,
     x_ref, lab_ref, nk_ref, heat_ref, op_ref, out_ref,
-    raw, eraw, eb, hb, s0, s1, s2, ex, ob, coef, op3,
-    a_send, a_recv, a_loc, z_send, z_recv, ze_send, ze_recv,
+    raw, eraw, eb, hb, s0, s1, s2, ex, ob, coef, op3, lab,
+    a_send, a_recv, a_loc, z_send, z_recv,
     h_send, h_recv, x_send, x_recv, o_send, o_recv, o_loc,
 ):
     d = lax.axis_index("depth")
@@ -75,16 +75,24 @@
             x_ref.at[:, :, block_cols(d, t)], raw.at[1, t, mine], a_loc.at[t]
         )
 
-    def forward(side, t):
+    def forward(side, j, t):
+        p = flipped(d, j, nd)
+        part = pl.ds(pl.multiple_of(p * layers_here, 8), layers_here)
         if t == tiles:
-            src, dst = eraw.at[1], eraw.at[2 - 2 * side]
-            snd, rcv = ze_send.at[side], ze_recv.at[side]
+            src, dst = eb.at[d] if j == 0 else eraw.at[1, part], eraw.at[2 - 2 * side, part]
         else:
-            src, dst = raw.at[1, t], raw.at[2 - 2 * side, t]
-            snd, rcv = z_send.at[side, t], z_recv.at[side, t]
+            src = x_ref.at[:, :, block_cols(d, t)] if j == 0 else raw.at[1, t, part]
+            dst = raw.at[2 - 2 * side, t, part]
         return pltpu.make_async_remote_copy(
-            src, dst, snd, rcv, device_id={"surf": near[side]}, device_id_type=MESH
-        )
+            src, dst, z_send.at[side, j, t], z_recv.at[side, j, t],
+            device_id={"surf": near[side]}, device_id_type=MESH,
+        )
+
+    def forward_both(j, t):
+        for side in range(2):
+            @pl.when(has[side])
+            def _():
+                forward(side, j, t).start()
 
     def heat_out(side):
         return pltpu.make_async_remote_copy(
@@ -115,6 +123,7 @@
 
     for j in peers:
         spread(j, 0).start()
+    forward_both(0, 0)
     lane8 = lax.broadcasted_iota(jnp.int32, (8, LANES), 1)
     for b in range(nd):
         @pl.loop(0, layers_here // 8)
@@ -134,6 +143,7 @@
     for t in [tiles] + list(range(1, tiles)):
         for j in peers:
             spread(j, t).start()
+        forward_both(0, t)
     for t in range(ring):
         keep(t).start()
     for side in range(2):
@@ -141,11 +151,16 @@
         def _():
             heat_out(side).start()
 
+    for b in range(layers // LANES):
+        row = lab_ref[:, b * LANES:(b + 1) * LANES].astype(jnp.float32)
+        tall = jnp.transpose(jnp.broadcast_to(row, (LANES, LANES)))
+        lab[b * LANES:(b + 1) * LANES, :] = tall
+
     @pl.loop(0, layers // 8)
     def _(g):
         rows = pl.ds(pl.multiple_of(g * 8, 8), 8)
-        lab = lab_ref[rows, :]
-        is0, is1, is2 = lab == 0, lab == 1, lab == 2
+        kind = lab[rows, :]
+        is0, is1, is2 = kind < 0.5, kind < 1.5, kind < 2.5
         total = jnp.zeros((8, LANES), jnp.float32)
         for k in range(24):
             c = jnp.where(
@@ -203,20 +218,19 @@
         @pl.loop(0, layers // 8)
         def _(g):
             rows = pl.ds(pl.multiple_of(g * 8, 8), 8)
-            cs = [coef[k, rows, :] for k in range(25)]
             acc = [None] * made
-            for i in range(made + 4):
-                mid, lo, hi = src[t, i, rows, :], src[left, i, rows, :], src[right, i, rows, :]
-                views = [
-                    pltpu.roll(jnp.where(lane8 >= LANES - 2, lo, mid), 2, 1),
-                    pltpu.roll(jnp.where(lane8 >= LANES - 1, lo, mid), 1, 1),
-                    mid,
-                    pltpu.roll(jnp.where(lane8 < 1, hi, mid), LANES - 1, 1),
-                    pltpu.roll(jnp.where(lane8 < 2, hi, mid), LANES - 2, 1),
-                ]
-                for r in range(max(0, i - 4), min(made, i + 1)):
-                    for q in range(5):
-                        term = cs[(i - r) * 5 + q] * views[q]
+            for q in (2, 1, 3, 0, 4):
+                cs = [coef[p * 5 + q, rows, :] for p in range(5)]
+                for i in range(made + 4):
+                    view = src[t, i, rows, :]
+                    if q < 2:
+                        view = jnp.where(lane8 >= LANES - 2 + q, src[left, i, rows, :], view)
+                        view = pltpu.roll(view, 2 - q, 1)
+                    elif q > 2:
+                        view = jnp.where(lane8 < q - 2, src[right, i, rows, :], view)
+                        view = pltpu.roll(view, LANES + 2 - q, 1)
+                    for r in range(max(0, i - 4), min(made, i + 1)):
+                        term = cs[i - r] * view
                         acc[r] = term if acc[r] is None else acc[r] + term
             for r in range(made):
                 ex[rows, r * LANES:(r + 1) * LANES] = acc[r]
@@ -262,11 +276,8 @@
             arrive(arrival[at - 1])
         for j in peers:
             spread(j, t).wait_recv()
+            forward_both(j, t)
         keep(t).wait()
-        for side in range(2):
-            @pl.when(has[side])
-            def _():
-                forward(side, t).start()
 
     @once
     def unpack(t):
@@ -294,7 +305,8 @@
         for side in range(2):
             @pl.when(has[side])
             def _():
-                forward(1 - side, t).wait_recv()
+                for j in range(nd):
+                    forward(1 - side, j, t).wait_recv()
                 relayout(2 * side)
 
     @once
@@ -358,7 +370,8 @@
         for side in range(2):
             @pl.when(has[side])
             def _():
-                forward(side, t).wait_send()
+                for j in range(nd):
+                    forward(side, j, t).wait_send()
                 trade(side, t).wait_send()
 
 
@@ -370,7 +383,7 @@
     layers = implicit_inverse_operator.shape[0]
     tiles = width // nd // LANES
     ring = tiles + 1
-    labels = jnp.broadcast_to(substance_label[:, None], (layers, LANES))
+    labels = substance_label[None, :]
     f32, dma = jnp.float32, pltpu.SemaphoreType.DMA
     vmem = pl.BlockSpec(memory_space=pltpu.VMEM)
     return pl.pallas_call(
@@ -390,8 +403,9 @@
             pltpu.VMEM((tiles, layers, rows, LANES), f32),
             pltpu.VMEM((25, layers, LANES), f32),
             pltpu.VMEM((layers, 3 * layers), jnp.bfloat16),
+            pltpu.VMEM((layers, LANES), f32),
             dma((nd, ring)), dma((nd, ring)), dma((ring,)),
-            dma((2, tiles)), dma((2, tiles)), dma((2,)), dma((2,)),
+            dma((2, nd, ring)), dma((2, nd, ring)),
             dma((2,)), dma((2,)), dma((2, ring)), dma((2, ring)),
             dma((nd, tiles)), dma((nd, tiles)), dma((tiles,)),
         ],

time: 124 us -> 120 us (0.968)
  Pallas kernels: 119 us -> 116 us
  local copies, waits for them, and re-layouts: 4.59 us -> 3.16 us
    pallas_call x1, Pallas kernels: 119 us -> 116 us  [shards(): pl.pallas_call(functools.partial(kernel, nd, ns, tiles), out_shape=jax.Sh...]
    broadcast_in_dim x1 -> x0, local copies, waits for them, and re-layouts: 1.43 us -> none  [shards(): labels = jnp.broadcast_to(substance_label[:, None], (layers, LANES))]
where the time goes in v2:
time: 120 us; the launch traced here: 119 us
  Pallas kernels  116 us (97%)
  local copies, waits for them, and re-layouts  3.16 us (3%)
    pallas_call x1, Pallas kernels, shards(): pl.pallas_call(functools.partial(kernel, nd, ns, tiles), out_shape=jax.Sh...  116 us
    unnamed x1, local copies, waits for them, and re-layouts  3.16 us

profile of v2, /device:TPU:16, one launch (start us, length us, event | category | flops | bytes accessed | tf_op | source)
XLA Modules:
  0.0 119.2 jit_solution(7692193589433752897)
XLA Ops:
  0.0 116.0 %shard_map.55 = f32[64,4,2048]{2,1,0:T(4,128)} custom-call(f32[64,4,2048]{2,1,0:T(4,128)} %x_ref.1, s32[1,256]{1,0:T(1,128)} %bitcast.1, f32[4,24]{1,0:T(4,128)} %nk_ref.1, f32[4,2048]{1,0:T(4,128)} %heat_ref.1, f32[256,256]{1,0:T(8,128)} %op_ref.1), custom_call_target="tpu_custom_call" | custom-call | tf_op jit(solution)/shard_map/pallas_call | solution.py:389
  116.0 3.2 %copy.7 = f32[64,4,2048]{2,1,0:T(4,128)} copy(f32[64,4,2048]{2,1,0:T(4,128)} %shard_map.55) | data formatting | bytes 4194304

commit v3 on v2

--- a/solution.py
+++ b/solution.py
@@ -215,7 +215,7 @@
     def lateral(src, t, made, first):
         left, right = (t - 1) % ring, (t + 1) % ring
 
-        @pl.loop(0, layers // 8)
+        @pl.loop(0, layers // 8, unroll=2)
         def _(g):
             rows = pl.ds(pl.multiple_of(g * 8, 8), 8)
             acc = [None] * made

time: 120 us -> 105 us (0.88)
  Pallas kernels: 116 us -> 102 us
    pallas_call x1, Pallas kernels: 116 us -> 102 us  [shards(): pl.pallas_call(functools.partial(kernel, nd, ns, tiles), out_shape=jax.Sh...]
where the time goes in v3:
time: 105 us
  Pallas kernels  102 us (97%)
  local copies, waits for them, and re-layouts  3.16 us (3%)
    pallas_call x1, Pallas kernels, shards(): pl.pallas_call(functools.partial(kernel, nd, ns, tiles), out_shape=jax.Sh...  102 us
    unnamed x1, local copies, waits for them, and re-layouts  3.16 us

profile of v3, /device:TPU:16, one launch (start us, length us, event | category | flops | bytes accessed | tf_op | source)
XLA Modules:
  0.0 105.1 jit_solution(7166066089742998308)
XLA Ops:
  0.0 102.0 %shard_map.55 = f32[64,4,2048]{2,1,0:T(4,128)} custom-call(f32[64,4,2048]{2,1,0:T(4,128)} %x_ref.1, s32[1,256]{1,0:T(1,128)} %bitcast.1, f32[4,24]{1,0:T(4,128)} %nk_ref.1, f32[4,2048]{1,0:T(4,128)} %heat_ref.1, f32[256,256]{1,0:T(8,128)} %op_ref.1), custom_call_target="tpu_custom_call" | custom-call | tf_op jit(solution)/shard_map/pallas_call | solution.py:389
  102.0 3.2 %copy.7 = f32[64,4,2048]{2,1,0:T(4,128)} copy(f32[64,4,2048]{2,1,0:T(4,128)} %shard_map.55) | data formatting | bytes 4194304

commit v4 on v3

--- a/solution.py
+++ b/solution.py
@@ -215,7 +215,7 @@
     def lateral(src, t, made, first):
         left, right = (t - 1) % ring, (t + 1) % ring
 
-        @pl.loop(0, layers // 8, unroll=2)
+        @pl.loop(0, layers // 8, unroll=4)
         def _(g):
             rows = pl.ds(pl.multiple_of(g * 8, 8), 8)
             acc = [None] * made

time: 105 us -> 98.4 us (0.937)
  Pallas kernels: 102 us -> 95 us
    pallas_call x1, Pallas kernels: 102 us -> 95 us  [shards(): pl.pallas_call(functools.partial(kernel, nd, ns, tiles), out_shape=jax.Sh...]
where the time goes in v4:
time: 98.4 us; the launch traced here: 98.2 us
  Pallas kernels  95 us (97%)
  local copies, waits for them, and re-layouts  3.16 us (3%)
    pallas_call x1, Pallas kernels, shards(): pl.pallas_call(functools.partial(kernel, nd, ns, tiles), out_shape=jax.Sh...  95 us
    unnamed x1, local copies, waits for them, and re-layouts  3.16 us

profile of v4, /device:TPU:16, one launch (start us, length us, event | category | flops | bytes accessed | tf_op | source)
XLA Modules:
  0.0 98.2 jit_solution(12815248708519905329)
XLA Ops:
  0.0 95.0 %shard_map.55 = f32[64,4,2048]{2,1,0:T(4,128)} custom-call(f32[64,4,2048]{2,1,0:T(4,128)} %x_ref.1, s32[1,256]{1,0:T(1,128)} %bitcast.1, f32[4,24]{1,0:T(4,128)} %nk_ref.1, f32[4,2048]{1,0:T(4,128)} %heat_ref.1, f32[256,256]{1,0:T(8,128)} %op_ref.1), custom_call_target="tpu_custom_call" | custom-call | tf_op jit(solution)/shard_map/pallas_call | solution.py:389
  95.0 3.2 %copy.7 = f32[64,4,2048]{2,1,0:T(4,128)} copy(f32[64,4,2048]{2,1,0:T(4,128)} %shard_map.55) | data formatting | bytes 4194304
